TPU v7x, 32 devices: a whole 2x2x4 slice. The times are simulated.
32 devices in a mesh: depth: 4 (over z), tile: 8 (over y, x, core).
Axes of the slice: x: 2, y: 2, z: 4, core: 2. Of those that a mesh axis runs over, the one named last changes fastest.
Arguments:
- patches: float32 [512, 64, 1024], P('tile', 'depth'), may hold values from 0.1 to 10
- patch_slot: int32 [512], P('tile'), may hold values from 0 to 511, as said below
Outputs:
- image: float32 [8, 64, 4, 1024], P('tile', 'depth')
Inputs may be any that keep to these rules, and one draw needn't show every extreme that they name: patch_slot is a permutation of the slots. Device s of tile (patches s * 64 to (s + 1) * 64 - 1) sends to owner t a number that depends only on (t - s) mod 8: one such difference, drawn from the seed, carries 24 patches, two carry none, the others 64 // 8. Every owner receives 64 patches.
All inputs are finite; a program needn't handle non-finite values.
Results may differ from a plain program's by a relative error of at most 0.00002.
Values sent between devices are 32-bit elements; how exact they have to be, the bound alone decides.
A program may use at most 128 MiB of HBM per device.

v0:
```python
import functools
import math

import jax
import jax.numpy as jnp
from jax import lax
from jax.experimental import pallas as pl
from jax.experimental.pallas import tpu as pltpu
from jax.sharding import PartitionSpec as P

BLOCK = 8
GROUPS = 2
LANES = 128
LABEL_ROWS = 8


def halos(patches):
    count = lax.axis_size("depth")
    forward = [(i, i + 1) for i in range(count - 1)]
    backward = [(target, source) for source, target in forward]
    low = lax.ppermute(jnp.log(patches[:, -1]), "depth", forward)
    high = lax.ppermute(jnp.log(patches[:, 0]), "depth", backward)
    return low, high


def shade_kernel(cells, scale, x_ref, low_ref, high_ref, out_ref):
    first = 0.6 * math.exp(-0.25) * scale
    second = 0.4 * math.exp(-2.0) * scale
    third = 0.3 * scale
    rows = GROUPS * BLOCK

    def plane(step, cell):
        base = step * (rows * cells) + cell
        return jnp.stack(
            [
                x_ref[pl.ds(base + group * BLOCK * cells, BLOCK, stride=cells), :]
                for group in range(GROUPS)
            ]
        )

    def patch_rows(step):
        return pl.ds(pl.multiple_of(step * rows, rows), rows)

    @pl.loop(0, low_ref.shape[0] // rows)
    def _(step):
        shape = (GROUPS, BLOCK, low_ref.shape[1])
        before = low_ref[patch_rows(step), :].reshape(shape)
        x = plane(step, 0)
        level = jnp.log(x)
        clear = jnp.ones_like(x)
        red = green = blue = jnp.zeros_like(x)
        for cell in range(cells):
            if cell + 1 < cells:
                x_after = plane(step, cell + 1)
                after = jnp.log(x_after)
            else:
                x_after, after = None, high_ref[patch_rows(step), :].reshape(shape)
            slope = (after - before) * 0.5
            slope2 = slope * slope
            square = x * x
            bell = jnp.exp(-level * level)
            wide = 1.0 + square
            below = wide * (1.0 + slope2)
            inverse = 1.0 / (square * below)
            ratio = bell * (inverse * below)
            optical = first * (bell * x) + second * (ratio * ratio) + third * slope2
            pass_on = jnp.exp(-optical)
            light = clear * (1.0 - pass_on) * (inverse * square)
            clear = clear * pass_on
            blue = blue + light
            red = red + light * square
            green = green + light * (bell * wide)
            before, level, x = level, after, x_after
        for c, value in enumerate((red, green, blue, clear)):
            out_ref[0, c, patch_rows(step), :] = value.reshape(rows, shape[2])


def shade(patches, low, high, quarters):
    per, cells, rays = patches.shape
    scale = 2.0 / (cells * quarters)
    width = rays // quarters
    halves = width // LANES
    return pl.pallas_call(
        functools.partial(shade_kernel, cells, scale),
        grid=(rays // LANES,),
        out_shape=jax.ShapeDtypeStruct((quarters, 4, per, width), jnp.float32),
        in_specs=[
            pl.BlockSpec((per * cells, LANES), lambda i: (0, i)),
            pl.BlockSpec((per, LANES), lambda i: (0, i)),
            pl.BlockSpec((per, LANES), lambda i: (0, i)),
        ],
        out_specs=pl.BlockSpec(
            (1, 4, per, LANES), lambda i: (i // halves, 0, 0, i % halves)
        ),
        name="shade",
    )(patches.reshape(per * cells, rays), low, high)


def composite(layers_ref, part):
    quarters = layers_ref.shape[0]
    color = [layers_ref[0, c] for c in range(3)]
    clear = layers_ref[0, 3]
    for depth in range(1, quarters):
        for c in range(3):
            color[c] = color[c] + clear * layers_ref[depth, c]
        clear = clear * layers_ref[depth, 3]
    return color + [clear]


def pack_kernel(tiles, slots, layers_ref, row_ref, col_ref, out_ref):
    per = row_ref.shape[1]
    width = out_ref.shape[2]
    row, col = row_ref[...], col_ref[...]
    shift = per.bit_length() - 1
    dest_row, dest_col = row >> shift, col >> shift
    same = (dest_col == dest_row).astype(jnp.float32)
    down = lax.broadcasted_iota(jnp.int32, (per, per), 0)
    across = lax.broadcasted_iota(jnp.int32, (per, per), 1)
    rank_row = jnp.sum(jnp.where(down < across, same, 0.0), axis=0, keepdims=True)
    rank_col = jnp.sum(jnp.where(across < down, same, 0.0), axis=1, keepdims=True)
    target_row = dest_row * slots + rank_row.astype(jnp.int32)
    target_col = dest_col * slots + rank_col.astype(jnp.int32)
    offset = (col & (per - 1)).astype(jnp.float32) + 1.0
    choice = (
        lax.broadcasted_iota(jnp.int32, (tiles * slots, per), 0) == target_row
    ).astype(jnp.float32)
    values = composite(layers_ref, None)
    for c in range(4):
        packed = jnp.dot(
            choice,
            values[c],
            precision=lax.Precision.HIGHEST,
            preferred_element_type=jnp.float32,
        )
        out_ref[:, c * slots : (c + 1) * slots, :] = packed.reshape(tiles, slots, width)
    lane = lax.broadcasted_iota(jnp.int32, (per, width), 1)
    for tile in range(tiles):
        hit = (target_col == tile * slots + lane) & (lane < slots)
        mark = jnp.sum(jnp.where(hit, offset, 0.0), axis=0, keepdims=True) - 1.0
        out_ref[tile, 4 * slots :, :] = jnp.broadcast_to(mark, (LABEL_ROWS, width))


def pack(layers, patch_slot, tiles, slots):
    per = patch_slot.shape[0]
    width = layers.shape[3]
    return pl.pallas_call(
        functools.partial(pack_kernel, tiles, slots),
        out_shape=jax.ShapeDtypeStruct((tiles, 4 * slots + LABEL_ROWS, width), jnp.float32),
        name="pack",
    )(layers, patch_slot.reshape(1, per), patch_slot.reshape(per, 1))


def place_kernel(slots, got_ref, out_ref):
    tiles, width = got_ref.shape[0], got_ref.shape[2]
    quarters, _, share, _ = out_ref.shape
    per = quarters * share
    place = lax.broadcasted_iota(jnp.int32, (per, slots), 0)
    totals = [jnp.zeros((per, width), jnp.float32) for _ in range(4)]
    for tile in range(tiles):
        mark = got_ref[tile, 4 * slots : 4 * slots + 1, :][:, :slots].astype(jnp.int32)
        choice = (place == mark).astype(jnp.float32)
        for c in range(4):
            totals[c] = totals[c] + jnp.dot(
                choice,
                got_ref[tile, c * slots : (c + 1) * slots, :],
                precision=lax.Precision.HIGHEST,
                preferred_element_type=jnp.float32,
            )
    totals[3] = 1.0 - totals[3]
    for c in range(4):
        out_ref[:, c] = totals[c].reshape(quarters, share, width)


def place(got, per, quarters, slots):
    width = got.shape[2]
    return pl.pallas_call(
        functools.partial(place_kernel, slots),
        out_shape=jax.ShapeDtypeStruct((quarters, 4, per // quarters, width), jnp.float32),
        name="place",
    )(got)


def swap(array, axis):
    return lax.all_to_all(array, axis, split_axis=0, concat_axis=0, tiled=True)


def local(patches, patch_slot):
    per, _, rays = patches.shape
    tiles = lax.axis_size("tile")
    quarters = lax.axis_size("depth")
    slots = -(-(3 * per // tiles) // 8) * 8
    low, high = halos(patches)
    layers = swap(shade(patches, low, high, quarters), "depth")
    got = swap(pack(layers, patch_slot, tiles, slots), "tile")
    final = swap(place(got, per, quarters, slots), "depth")
    return final.transpose(2, 1, 0, 3).reshape(1, per // quarters, 4, rays)


def solution(mesh):
    return jax.shard_map(
        local,
        mesh=mesh,
        in_specs=(P("tile", "depth", None), P("tile")),
        out_specs=P("tile", "depth", None, None),
        check_vma=False,
    )
```

profile of v0, /device:TPU:0, one launch (start us, length us, event | category | flops | bytes accessed | tf_op | source)
XLA Modules:
  0.0 94.4 jit_solution(7713170071577398533)
XLA Ops:
  0.0 2.7 %fusion.2 = (f32[64,1,1024]{2,1,0:T(1,128)S(1)}, f32[64,1,1024]{2,1,0:T(1,128)S(1)}) fusion(f32[64,16,1024]{2,1,0:T(8,128)} %param.2), kind=kLoop, calls=%fused_computation.4 | loop fusion | bytes 1048576 | tf_op jit(solution)/shard_map/slice | solution.py:22
  2.8 0.1 fusion.1
  2.8 5.0 %collective-permute-start = (f32[64,1024]{1,0:T(8,128)S(1)}, f32[64,1024]{1,0:T(8,128)S(1)}, u32[]{:S(2)}, u32[]{:S(2)}) collective-permute-start(f32[64,1024]{1,0:T(8,128)S(1)} %fusion.1), channel_id=1, source_target_pairs={{0,8},{8,16},{16,24},{1,9},{9,17},{17,25},{2,10},{10,18},{18,26},{... | collective-permute-start | bytes 786440 | tf_op jit(solution)/shard_map/ppermute | solution.py:21
  7.8 0.0 copy-start.3
  7.8 0.1 fusion
  7.9 1.3 %collective-permute-start.1 = (f32[64,1024]{1,0:T(8,128)S(1)}, f32[64,1024]{1,0:T(8,128)S(1)}, u32[]{:S(2)}, u32[]{:S(2)}) collective-permute-start(f32[64,1024]{1,0:T(8,128)S(1)} %fusion), channel_id=1, source_target_pairs={{8,0},{16,8},{24,16},{9,1},{17,9},{25,17},{10,2},{18,10},{26,18},{... | collective-permute-start | bytes 786440 | tf_op jit(solution)/shard_map/ppermute | solution.py:22
  9.2 4.2 %collective-permute-done.low_ref = f32[64,1024]{1,0:T(8,128)S(1)} collective-permute-done((f32[64,1024]{1,0:T(8,128)S(1)}, f32[64,1024]{1,0:T(8,128)S(1)}, u32[]{:S(2)}, u32[]{:S(2)}) %collective-permute-start) | collective-permute-done | bytes 262176 | tf_op jit(solution)/shard_map/ppermute | solution.py:21
  13.3 0.0 copy-start.1
  13.3 4.2 %collective-permute-done.1.high_ref = f32[64,1024]{1,0:T(8,128)S(1)} collective-permute-done((f32[64,1024]{1,0:T(8,128)S(1)}, f32[64,1024]{1,0:T(8,128)S(1)}, u32[]{:S(2)}, u32[]{:S(2)}) %collective-permute-start.1) | collective-permute-done | bytes 262176 | tf_op jit(solution)/shard_map/ppermute | solution.py:22
  17.5 0.0 copy-start.2
  17.5 0.0 copy-done.1
  17.5 0.7 copy-done.2
  18.3 9.2 %shade.1 = f32[4,4,64,256]{3,2,1,0:T(8,128)} custom-call(f32[1024,1024]{1,0:T(8,128)} %bitcast.8, f32[64,1024]{1,0:T(8,128)} %copy-done.1, f32[64,1024]{1,0:T(8,128)} %copy-done.2), custom_call_target="tpu_custom_call" | custom-call | tf_op jit(solution)/shard_map/shade/pallas_call | solution.py:83
  27.4 3.8 %all-to-all-start = ((f32[4,4,64,256]{3,2,1,0:T(8,128)}), f32[4,4,64,256]{3,2,1,0:T(8,128)S(1)}, u32[]{:S(2)}, u32[]{:S(2)}) async-start(f32[4,4,64,256]{3,2,1,0:T(8,128)} %shade.1), calls=%async_computation | async-start | bytes 2097152 | tf_op jit(solution)/shard_map/all_to_all | solution.py:184
  31.3 0.0 copy-done.3
  31.3 0.7 copy.8.col_ref
  32.0 23.9 %all-to-all-done.layers_ref = f32[4,4,64,256]{3,2,1,0:T(8,128)S(1)} async-done(((f32[4,4,64,256]{3,2,1,0:T(8,128)}), f32[4,4,64,256]{3,2,1,0:T(8,128)S(1)}, u32[]{:S(2)}, u32[]{:S(2)}) %all-to-all-start) | async-done | bytes 1048608 | tf_op jit(solution)/shard_map/all_to_all | solution.py:184
  55.9 0.0 copy-start
  55.9 1.0 %copy-done = f32[4,4,64,256]{3,2,1,0:T(8,128)} copy-done((f32[4,4,64,256]{3,2,1,0:T(8,128)}, f32[4,4,64,256]{3,2,1,0:T(8,128)S(1)}, u32[]{:S(2)}) %copy-start) | copy-done | bytes 1048600
  56.8 3.0 %pack.1 = f32[8,104,256]{2,1,0:T(8,128)} custom-call(f32[4,4,64,256]{3,2,1,0:T(8,128)} %copy-done, s32[1,64]{1,0:T(1,128)} %bitcast.10, s32[64,1]{1,0:T(8,128)} %copy.8.col_ref), custom_call_target="tpu_custom_call" | custom-call | tf_op jit(solution)/shard_map/pack/pallas_call | solution.py:146
  59.9 17.4 %all_to_all.15.got_ref = f32[8,104,256]{2,1,0:T(8,128)} all-to-all(f32[8,104,256]{2,1,0:T(8,128)} %pack.1), channel_id=1, replica_groups=mesh['depth'=4,'tile'=8] {'tile'}, dimensions={0} | all-to-all | bytes 1703936 | tf_op jit(solution)/shard_map/all_to_all | solution.py:184
  77.3 3.6 %place.1 = f32[4,4,16,256]{3,2,1,0:T(8,128)} custom-call(f32[8,104,256]{2,1,0:T(8,128)} %all_to_all.15.got_ref), custom_call_target="tpu_custom_call" | custom-call | tf_op jit(solution)/shard_map/place/pallas_call | solution.py:176
  80.9 12.4 %all_to_all.16 = f32[4,4,16,256]{3,2,1,0:T(8,128)S(1)} all-to-all(f32[4,4,16,256]{3,2,1,0:T(8,128)} %place.1), channel_id=1, replica_groups=mesh['depth'=4,'tile'=8] {'depth'}, dimensions={0} | all-to-all | bytes 524288 | tf_op jit(solution)/shard_map/all_to_all | solution.py:184
  93.4 0.2 copy.11
  93.6 0.9 reshape.18
Async XLA Ops:
  2.8 10.5 %collective-permute-start = (f32[64,1024]{1,0:T(8,128)S(1)}, f32[64,1024]{1,0:T(8,128)S(1)}, u32[]{:S(2)}, u32[]{:S(2)}) collective-permute-start(f32[64,1024]{1,0:T(8,128)S(1)} %fusion.1), channel_id=1, source_target_pairs={{0,8},{8,16},{16,24},{1,9},{9,17},{17,25},{2,10},{10,18},{18,26},{... | collective-permute-start | bytes 786440 | tf_op jit(solution)/shard_map/ppermute | solution.py:21
  7.8 23.5 %copy-start.3 = (s32[64]{0:T(128)S(1)}, s32[64]{0:T(128)}, u32[]{:S(2)}) copy-start(s32[64]{0:T(128)} %param.3) | copy-start | bytes 772
  7.9 9.7 %collective-permute-start.1 = (f32[64,1024]{1,0:T(8,128)S(1)}, f32[64,1024]{1,0:T(8,128)S(1)}, u32[]{:S(2)}, u32[]{:S(2)}) collective-permute-start(f32[64,1024]{1,0:T(8,128)S(1)} %fusion), channel_id=1, source_target_pairs={{8,0},{16,8},{24,16},{9,1},{17,9},{25,17},{10,2},{18,10},{26,18},{... | collective-permute-start | bytes 786440 | tf_op jit(solution)/shard_map/ppermute | solution.py:22
  13.3 4.2 %copy-start.1 = (f32[64,1024]{1,0:T(8,128)}, f32[64,1024]{1,0:T(8,128)S(1)}, u32[]{:S(2)}) copy-start(f32[64,1024]{1,0:T(8,128)S(1)} %collective-permute-done.low_ref) | copy-start | bytes 786436
  17.5 0.7 copy-start.2
  27.4 28.4 %all-to-all-start = ((f32[4,4,64,256]{3,2,1,0:T(8,128)}), f32[4,4,64,256]{3,2,1,0:T(8,128)S(1)}, u32[]{:S(2)}, u32[]{:S(2)}) async-start(f32[4,4,64,256]{3,2,1,0:T(8,128)} %shade.1), calls=%async_computation | async-start | bytes 2097152 | tf_op jit(solution)/shard_map/all_to_all | solution.py:184
  55.9 1.0 %copy-start = (f32[4,4,64,256]{3,2,1,0:T(8,128)}, f32[4,4,64,256]{3,2,1,0:T(8,128)S(1)}, u32[]{:S(2)}) copy-start(f32[4,4,64,256]{3,2,1,0:T(8,128)S(1)} %all-to-all-done.layers_ref) | copy-start | bytes 3145732
where the time goes:
time: 95 us; the launch traced here: 94.4 us
  waiting for transfers between devices  32.2 us (34%)
  blocking collectives  29.9 us (31%)
  Pallas kernels  15.9 us (17%)
  starting transfers between devices  10.1 us (11%)
  local copies, waits for them, and re-layouts  6.31 us (7%)
    all_to_all x2, blocking collectives, swap(): return lax.all_to_all(array, axis, split_axis=0, concat_axis=0, tiled=True)  29.9 us
    all_to_all x1, waiting for transfers between devices, swap(): return lax.all_to_all(array, axis, split_axis=0, concat_axis=0, tiled=True)  23.9 us
    pallas_call x1, Pallas kernels, shade(): pl.pallas_call(functools.partial(shade_kernel, cells, scale), grid=(rays...  9.17 us
    ppermute x1, starting transfers between devices, halos(): low = lax.ppermute(jnp.log(patches[:, -1]), 'depth', forward)  4.97 us
    ppermute x1, waiting for transfers between devices, halos(): high = lax.ppermute(jnp.log(patches[:, 0]), 'depth', backward)  4.21 us
    ppermute x1, waiting for transfers between devices, halos(): low = lax.ppermute(jnp.log(patches[:, -1]), 'depth', forward)  4.15 us
    all_to_all x1, starting transfers between devices, swap(): return lax.all_to_all(array, axis, split_axis=0, concat_axis=0, tiled=True)  3.85 us
    pallas_call x1, Pallas kernels, place(): pl.pallas_call(functools.partial(place_kernel, slots), out_shape=jax.Shap...  3.63 us
  transfers between devices with their start and end apart: 3, of which 3 were waited for; matrix products, arithmetic and copies ran while one was open for 1% of the time, Pallas kernels for 0%

commit v1 on v0

v1 whole, which is shorter than its diff:
```python
import functools
import math

import jax
import jax.numpy as jnp
from jax import lax
from jax.experimental import pallas as pl
from jax.experimental.pallas import tpu as pltpu
from jax.sharding import PartitionSpec as P

BLOCK = 8
GROUPS = 2
LANES = 128
MESH = pl.DeviceIdType.MESH
LABEL_ROWS = 8


def ray_cell(scale, state, x, before, level, after):
    red, green, blue, clear = state
    slope = (after - before) * 0.5
    slope2 = slope * slope
    square = x * x
    bell = jnp.exp(-level * level)
    wide = 1.0 + square
    below = wide * (1.0 + slope2)
    inverse = 1.0 / (square * below)
    ratio = bell * (inverse * below)
    optical = (
        (0.6 * math.exp(-0.25) * scale) * (bell * x)
        + (0.4 * math.exp(-2.0) * scale) * (ratio * ratio)
        + (0.3 * scale) * slope2
    )
    pass_on = jnp.exp(-optical)
    light = clear * (1.0 - pass_on) * (inverse * square)
    return (
        red + light * square,
        green + light * (bell * wide),
        blue + light,
        clear * pass_on,
    )


def over(front, back):
    clear = front[3]
    return tuple(front[c] + clear * back[c] for c in range(3)) + (clear * back[3],)


def greet(peers):
    barrier = pltpu.get_barrier_semaphore()
    for peer in peers:
        pl.semaphore_signal(barrier, inc=1, device_id=peer, device_id_type=MESH)
    pl.semaphore_wait(barrier, len(peers))


def front_kernel(
    cells, quarters, scale, x_hbm, out_ref,
    x_ref, edge, halo, part, got, load_sem, edge_send, edge_recv, send_sem, recv_sem,
):
    me = lax.axis_index("depth")
    _, per, width = out_ref.shape
    halves = width // LANES
    chunks = quarters * halves
    rows = GROUPS * BLOCK
    shape = (GROUPS, BLOCK, LANES)
    loads = [
        pltpu.make_async_copy(
            x_hbm.at[:, pl.ds(j * LANES, LANES)], x_ref.at[j], load_sem.at[j]
        )
        for j in range(chunks)
    ]
    for load in loads:
        load.start()
    greet([{"depth": lax.rem(me + k, quarters)} for k in range(1, quarters)])

    def plane(chunk, step, cell):
        base = step * (rows * cells) + cell
        return jnp.stack(
            [
                x_ref[chunk, pl.ds(base + g * BLOCK * cells, BLOCK, stride=cells), :]
                for g in range(GROUPS)
            ]
        )

    def patch_rows(step):
        return pl.ds(pl.multiple_of(step * rows, rows), rows)

    for j in range(chunks):
        loads[j].wait()

        @pl.loop(0, per // rows)
        def _(step):
            for side, cell in enumerate((0, cells - 1)):
                value = jnp.log(plane(j, step, cell)).reshape(rows, LANES)
                edge[side, patch_rows(step), pl.ds(j * LANES, LANES)] = value

    def edge_copy(side, source, peer):
        return pltpu.make_async_remote_copy(
            src_ref=edge.at[source],
            dst_ref=halo.at[side],
            send_sem=edge_send.at[side],
            recv_sem=edge_recv.at[side],
            device_id={"depth": peer},
            device_id_type=MESH,
        )

    up = edge_copy(0, 1, lax.rem(me + 1, quarters))
    down = edge_copy(1, 0, lax.rem(me + quarters - 1, quarters))

    @pl.when(me < quarters - 1)
    def _():
        up.start()

    @pl.when(me > 0)
    def _():
        down.start()

    @pl.when(me == 0)
    def _():
        halo[0] = jnp.zeros_like(halo[0])

    @pl.when(me == quarters - 1)
    def _():
        halo[1] = jnp.zeros_like(halo[1])

    ones = functools.partial(jnp.ones, shape, jnp.float32)
    zeros = functools.partial(jnp.zeros, shape, jnp.float32)

    @pl.loop(0, chunks)
    def _(chunk):
        quarter = chunk // halves
        lanes = pl.ds(pl.multiple_of((chunk % halves) * LANES, LANES), LANES)

        @pl.loop(0, per // rows)
        def _(step):
            before = jnp.log(plane(chunk, step, 0))
            x = plane(chunk, step, 1)
            level = jnp.log(x)
            state = (zeros(), zeros(), zeros(), ones())
            for cell in range(1, cells - 1):
                x_after = plane(chunk, step, cell + 1)
                after = jnp.log(x_after)
                state = ray_cell(scale, state, x, before, level, after)
                before, level, x = level, after, x_after
            for c in range(4):
                part[quarter, c, patch_rows(step), lanes] = state[c].reshape(rows, LANES)

    @pl.when(me > 0)
    def _():
        up.wait_recv()

    @pl.when(me < quarters - 1)
    def _():
        down.wait_recv()

    def piece(quarter, source, peer):
        return pltpu.make_async_remote_copy(
            src_ref=part.at[quarter],
            dst_ref=got.at[source],
            send_sem=send_sem.at[peer],
            recv_sem=recv_sem.at[source],
            device_id={"depth": peer},
            device_id_type=MESH,
        )

    def finish(quarter, store):
        for half in range(halves):
            chunk = quarter * halves + half
            lanes = pl.ds(half * LANES, LANES)
            wide = pl.ds(pl.multiple_of(chunk * LANES, LANES), LANES)

            @pl.loop(0, per // rows)
            def _(step):
                start = (zeros(), zeros(), zeros(), ones())
                x = plane(chunk, step, 0)
                first = ray_cell(
                    scale, start, x,
                    halo[0, patch_rows(step), wide].reshape(shape),
                    jnp.log(x),
                    jnp.log(plane(chunk, step, 1)),
                )
                x = plane(chunk, step, cells - 1)
                last = ray_cell(
                    scale, start, x,
                    jnp.log(plane(chunk, step, cells - 2)),
                    jnp.log(x),
                    halo[1, patch_rows(step), wide].reshape(shape),
                )
                inner = tuple(
                    part[quarter, c, patch_rows(step), lanes].reshape(shape)
                    for c in range(4)
                )
                total = over(over(first, inner), last)
                for c in range(4):
                    store(c, patch_rows(step), lanes, total[c].reshape(rows, LANES))

    for k in range(1, quarters):
        target = lax.rem(me + k, quarters)

        def keep(c, at, lanes, value, target=target):
            part[target, c, at, lanes] = value

        finish(target, keep)
        piece(target, me, target).start()

    def own(c, at, lanes, value):
        got[me, c, at, lanes] = value

    finish(me, own)
    for k in range(1, quarters):
        source = lax.rem(me + k, quarters)
        piece(me, source, source).wait_recv()
    total = tuple(got[0, c] for c in range(4))
    for depth in range(1, quarters):
        total = over(total, tuple(got[depth, c] for c in range(4)))
    for c in range(4):
        out_ref[c] = total[c]
    for k in range(1, quarters):
        target = lax.rem(me + k, quarters)
        piece(target, me, target).wait_send()

    @pl.when(me < quarters - 1)
    def _():
        up.wait_send()

    @pl.when(me > 0)
    def _():
        down.wait_send()


def front(patches, quarters):
    per, cells, rays = patches.shape
    width = rays // quarters
    chunks = rays // LANES
    dma = pltpu.SemaphoreType.DMA
    return pl.pallas_call(
        functools.partial(front_kernel, cells, quarters, 2.0 / (cells * quarters)),
        out_shape=jax.ShapeDtypeStruct((4, per, width), jnp.float32),
        in_specs=[pl.BlockSpec(memory_space=pl.ANY)],
        out_specs=pl.BlockSpec(memory_space=pltpu.VMEM),
        scratch_shapes=[
            pltpu.VMEM((chunks, per * cells, LANES), jnp.float32),
            pltpu.VMEM((2, per, rays), jnp.float32),
            pltpu.VMEM((2, per, rays), jnp.float32),
            pltpu.VMEM((quarters, 4, per, width), jnp.float32),
            pltpu.VMEM((quarters, 4, per, width), jnp.float32),
            dma((chunks,)),
            dma((2,)),
            dma((2,)),
            dma((quarters,)),
            dma((quarters,)),
        ],
        compiler_params=pltpu.CompilerParams(collective_id=0, has_side_effects=True),
        name="front",
    )(patches.reshape(per * cells, rays))


def pack(tiles, slots, values_ref, row_ref, col_ref, out_ref):
    per = row_ref.shape[1]
    width = out_ref.shape[2]
    row, col = row_ref[...], col_ref[...]
    shift = per.bit_length() - 1
    dest_row, dest_col = row >> shift, col >> shift
    same = (dest_col == dest_row).astype(jnp.float32)
    down = lax.broadcasted_iota(jnp.int32, (per, per), 0)
    across = lax.broadcasted_iota(jnp.int32, (per, per), 1)
    rank_row = jnp.sum(jnp.where(down < across, same, 0.0), axis=0, keepdims=True)
    rank_col = jnp.sum(jnp.where(across < down, same, 0.0), axis=1, keepdims=True)
    target_row = dest_row * slots + rank_row.astype(jnp.int32)
    target_col = dest_col * slots + rank_col.astype(jnp.int32)
    offset = (col & (per - 1)).astype(jnp.float32) + 1.0
    choice = (
        lax.broadcasted_iota(jnp.int32, (tiles * slots, per), 0) == target_row
    ).astype(jnp.float32)
    for c in range(4):
        packed = jnp.dot(
            choice,
            values_ref[c],
            precision=lax.Precision.HIGHEST,
            preferred_element_type=jnp.float32,
        )
        out_ref[:, c * slots : (c + 1) * slots, :] = packed.reshape(tiles, slots, width)
    lane = lax.broadcasted_iota(jnp.int32, (per, width), 1)
    for tile in range(tiles):
        hit = (target_col == tile * slots + lane) & (lane < slots)
        mark = jnp.sum(jnp.where(hit, offset, 0.0), axis=0, keepdims=True) - 1.0
        out_ref[tile, 4 * slots :, :] = jnp.broadcast_to(mark, (LABEL_ROWS, width))


def place(slots, got_ref, out_ref):
    tiles, width = got_ref.shape[0], got_ref.shape[2]
    quarters, _, share, _ = out_ref.shape
    per = quarters * share
    at = lax.broadcasted_iota(jnp.int32, (per, slots), 0)
    totals = [jnp.zeros((per, width), jnp.float32) for _ in range(4)]
    for tile in range(tiles):
        mark = got_ref[tile, 4 * slots : 4 * slots + 1, :][:, :slots].astype(jnp.int32)
        choice = (at == mark).astype(jnp.float32)
        for c in range(4):
            totals[c] = totals[c] + jnp.dot(
                choice,
                got_ref[tile, c * slots : (c + 1) * slots, :],
                precision=lax.Precision.HIGHEST,
                preferred_element_type=jnp.float32,
            )
    totals[3] = 1.0 - totals[3]
    for c in range(4):
        out_ref[:, c] = totals[c].reshape(quarters, share, width)


def exchange(axis, count, source_ref, got_ref, send_sem, recv_sem):
    me = lax.axis_index(axis)

    def copy(piece, source, peer):
        return pltpu.make_async_remote_copy(
            src_ref=source_ref.at[piece],
            dst_ref=got_ref.at[source],
            send_sem=send_sem.at[peer],
            recv_sem=recv_sem.at[source],
            device_id={axis: peer},
            device_id_type=MESH,
        )

    peers = [lax.rem(me + k, count) for k in range(1, count)]
    for peer in peers:
        copy(peer, me, peer).start()
    got_ref[me] = source_ref[me]
    for peer in peers:
        copy(me, peer, peer).wait_recv()
    for peer in peers:
        copy(peer, me, peer).wait_send()


def back_kernel(
    tiles, quarters, slots, values_ref, row_ref, col_ref, out_ref,
    packed, got, placed, landed, tile_send, tile_recv, depth_send, depth_recv,
):
    peers = [
        {axis: lax.rem(lax.axis_index(axis) + k, count)}
        for axis, count in (("tile", tiles), ("depth", quarters))
        for k in range(1, count)
    ]
    greet(peers)
    pack(tiles, slots, values_ref, row_ref, col_ref, packed)
    exchange("tile", tiles, packed, got, tile_send, tile_recv)
    place(slots, got, placed)
    exchange("depth", quarters, placed, landed, depth_send, depth_recv)
    out_ref[...] = landed[...]


def back(values, patch_slot, tiles, quarters, slots):
    _, per, width = values.shape
    dma = pltpu.SemaphoreType.DMA
    result = (quarters, 4, per // quarters, width)
    block = (tiles, 4 * slots + LABEL_ROWS, width)
    return pl.pallas_call(
        functools.partial(back_kernel, tiles, quarters, slots),
        out_shape=jax.ShapeDtypeStruct(result, jnp.float32),
        in_specs=[pl.BlockSpec(memory_space=pltpu.VMEM)] * 3,
        out_specs=pl.BlockSpec(memory_space=pltpu.VMEM),
        scratch_shapes=[
            pltpu.VMEM(block, jnp.float32),
            pltpu.VMEM(block, jnp.float32),
            pltpu.VMEM(result, jnp.float32),
            pltpu.VMEM(result, jnp.float32),
            dma((tiles,)),
            dma((tiles,)),
            dma((quarters,)),
            dma((quarters,)),
        ],
        compiler_params=pltpu.CompilerParams(collective_id=1, has_side_effects=True),
        name="back",
    )(values, patch_slot.reshape(1, per), patch_slot.reshape(per, 1))


def local(patches, patch_slot):
    per, _, rays = patches.shape
    tiles = lax.axis_size("tile")
    quarters = lax.axis_size("depth")
    slots = -(-(3 * per // tiles) // 8) * 8
    values = front(patches, quarters)
    final = back(values, patch_slot, tiles, quarters, slots)
    return final.transpose(2, 1, 0, 3).reshape(1, per // quarters, 4, rays)


def solution(mesh):
    return jax.shard_map(
        local,
        mesh=mesh,
        in_specs=(P("tile", "depth", None), P("tile")),
        out_specs=P("tile", "depth", None, None),
        check_vma=False,
    )
```

time: 95 us -> 63.8 us (0.67)
  Pallas kernels: 15.9 us -> 60.3 us
  waiting for transfers between devices: 32.2 us -> 0 us
  blocking collectives: 29.9 us -> 0 us
  starting transfers between devices: 10.1 us -> 0 us
  local copies, waits for them, and re-layouts: 6.31 us -> 3.36 us
    pallas_call x3 -> x2, Pallas kernels: 15.9 us -> 60.3 us  [the longest x1 32.5 us: front(): pl.pallas_call(functools.partial(front_kernel, cells, quarters, 2.0 / (ce...]
    all_to_all x2 -> x0, blocking collectives: 29.9 us -> none  [swap(): return lax.all_to_all(array, axis, split_axis=0, concat_axis=0, tiled=True)]
    all_to_all x1 -> x0, waiting for transfers between devices: 23.9 us -> none  [swap(): return lax.all_to_all(array, axis, split_axis=0, concat_axis=0, tiled=True)]
    ppermute x2 -> x0, waiting for transfers between devices: 8.36 us -> none  [the longest x1 4.21 us: halos(): high = lax.ppermute(jnp.log(patches[:, 0]), 'depth', backward)]
    ppermute x2 -> x0, starting transfers between devices: 6.26 us -> none  [the longest x1 4.97 us: halos(): low = lax.ppermute(jnp.log(patches[:, -1]), 'depth', forward)]
    all_to_all x1 -> x0, starting transfers between devices: 3.85 us -> none  [swap(): return lax.all_to_all(array, axis, split_axis=0, concat_axis=0, tiled=True)]
    slice x1 -> x0, local copies, waits for them, and re-layouts: 2.74 us -> none  [halos(): high = lax.ppermute(jnp.log(patches[:, 0]), 'depth', backward)]
    unnamed x8 -> x0, local copies, waits for them, and re-layouts: 1.69 us -> none
  transfers between devices with their start and end apart: 3 -> 0, of which waited for: 3 -> 0; matrix products, arithmetic and copies ran while one was open for 1% -> 0% of each run, Pallas kernels for 0% -> 0%
where the time goes in v1:
time: 63.8 us; the launch traced here: 63.7 us
  Pallas kernels  60.3 us (95%)
  local copies, waits for them, and re-layouts  3.36 us (5%)
    pallas_call x1, Pallas kernels, front(): pl.pallas_call(functools.partial(front_kernel, cells, quarters, 2.0 / (ce...  32.5 us
    pallas_call x1, Pallas kernels, back(): pl.pallas_call(functools.partial(back_kernel, tiles, quarters, slots), ou...  27.8 us
    reshape x2, local copies, waits for them, and re-layouts, local(): return final.transpose(2, 1, 0, 3).reshape(1, per // quarters, 4, rays)  2.01 us
    reshape x1, local copies, waits for them, and re-layouts, back(): patch_slot.reshape(per, 1)  1.36 us

profile of v1, /device:TPU:0, one launch (start us, length us, event | category | flops | bytes accessed | tf_op | source)
XLA Modules:
  0.0 63.7 jit_solution(9241535399680176194)
XLA Ops:
  0.0 1.4 %copy.4.col_ref = s32[64,1]{1,0:T(8,128)} copy(s32[64,1]{0,1:T(1,128)} %bitcast.6) | data formatting | bytes 512 | tf_op jit(solution)/shard_map/reshape | solution.py:372
  1.4 32.5 %front.1.values_ref = f32[4,64,256]{2,1,0:T(8,128)} custom-call(f32[1024,1024]{1,0:T(8,128)} %bitcast.4), custom_call_target="tpu_custom_call" | custom-call | tf_op jit(solution)/shard_map/front/pallas_call | solution.py:235
  33.9 27.8 %back.1 = f32[4,4,16,256]{3,2,1,0:T(8,128)} custom-call(f32[4,64,256]{2,1,0:T(8,128)} %front.1.values_ref, s32[1,64]{1,0:T(1,128)} %bitcast.7, s32[64,1]{1,0:T(8,128)} %copy.4.col_ref), custom_call_target="tpu_custom_call" | custom-call | tf_op jit(solution)/shard_map/back/pallas_call | solution.py:355
  61.7 1.1 %copy.7 = f32[16,4,4,256]{3,2,1,0:T(4,128)S(1)} copy(f32[16,4,4,256]{3,0,1,2:T(8,128)} %bitcast.5) | data formatting | bytes 524288 | tf_op jit(solution)/shard_map/reshape | solution.py:382
  62.8 0.9 %reshape.16 = f32[1,16,4,1024]{3,2,1,0:T(4,128)} reshape(f32[16,4,4,256]{3,2,1,0:T(4,128)S(1)} %copy.7) | data formatting | bytes 524288 | tf_op jit(solution)/shard_map/reshape | solution.py:382

commit v2 on v1

--- a/solution.py
+++ b/solution.py
@@ -152,17 +152,18 @@
     def _():
         down.wait_recv()
 
-    def piece(quarter, source, peer):
+    def hop(side, quarter):
+        peer = lax.rem(me + (quarters - 1 if side else 1), quarters)
         return pltpu.make_async_remote_copy(
             src_ref=part.at[quarter],
-            dst_ref=got.at[source],
-            send_sem=send_sem.at[peer],
-            recv_sem=recv_sem.at[source],
+            dst_ref=got.at[side, quarter],
+            send_sem=send_sem.at[side, quarter],
+            recv_sem=recv_sem.at[side, quarter],
             device_id={"depth": peer},
             device_id_type=MESH,
         )
 
-    def finish(quarter, store):
+    def finish(quarter):
         for half in range(halves):
             chunk = quarter * halves + half
             lanes = pl.ds(half * LANES, LANES)
@@ -191,32 +192,56 @@
                 )
                 total = over(over(first, inner), last)
                 for c in range(4):
-                    store(c, patch_rows(step), lanes, total[c].reshape(rows, LANES))
-
-    for k in range(1, quarters):
-        target = lax.rem(me + k, quarters)
-
-        def keep(c, at, lanes, value, target=target):
-            part[target, c, at, lanes] = value
-
-        finish(target, keep)
-        piece(target, me, target).start()
-
-    def own(c, at, lanes, value):
-        got[me, c, at, lanes] = value
-
-    finish(me, own)
-    for k in range(1, quarters):
-        source = lax.rem(me + k, quarters)
-        piece(me, source, source).wait_recv()
-    total = tuple(got[0, c] for c in range(4))
-    for depth in range(1, quarters):
-        total = over(total, tuple(got[depth, c] for c in range(4)))
+                    part[quarter, c, patch_rows(step), lanes] = total[c].reshape(rows, LANES)
+
+    last = quarters - 1
+    near = (me < quarters // 2).astype(jnp.int32)
+    for k in range(quarters):
+        quarter = k + near * (last - 2 * k)
+        finish(quarter)
+        if k < last:
+            for side, end in enumerate((0, last)):
+                @pl.when(me == end)
+                def _():
+                    hop(side, last - k if side == 0 else k).start()
+
+    def merge(side, quarter):
+        own = tuple(part[quarter, c] for c in range(4))
+        come = tuple(got[side, quarter, c] for c in range(4))
+        total = over(own, come) if side else over(come, own)
+        for c in range(4):
+            part[quarter, c] = total[c]
+
+    def turn(side, t):
+        rank = last - me if side else me
+        quarter = t - rank if side else last - t + rank
+        return rank, quarter
+
+    for t in range(1, last):
+        for side in (0, 1):
+            rank, quarter = turn(side, t)
+
+            @pl.when((rank >= 1) & (rank <= t))
+            def _():
+                hop(side, quarter).wait_recv()
+                merge(side, quarter)
+                hop(side, quarter).start()
+
+    for side, end in enumerate((0, last)):
+        @pl.when(me != end)
+        def _():
+            hop(side, me).wait_recv()
+            merge(side, me)
+
     for c in range(4):
-        out_ref[c] = total[c]
-    for k in range(1, quarters):
-        target = lax.rem(me + k, quarters)
-        piece(target, me, target).wait_send()
+        out_ref[c] = part[me, c]
+    for t in range(last):
+        for side in (0, 1):
+            rank, quarter = turn(side, t)
+
+            @pl.when(rank <= t)
+            def _():
+                hop(side, quarter).wait_send()
 
     @pl.when(me < quarters - 1)
     def _():
@@ -242,21 +267,21 @@
             pltpu.VMEM((2, per, rays), jnp.float32),
             pltpu.VMEM((2, per, rays), jnp.float32),
             pltpu.VMEM((quarters, 4, per, width), jnp.float32),
-            pltpu.VMEM((quarters, 4, per, width), jnp.float32),
+            pltpu.VMEM((2, quarters, 4, per, width), jnp.float32),
             dma((chunks,)),
             dma((2,)),
             dma((2,)),
-            dma((quarters,)),
-            dma((quarters,)),
+            dma((2, quarters)),
+            dma((2, quarters)),
         ],
         compiler_params=pltpu.CompilerParams(collective_id=0, has_side_effects=True),
         name="front",
     )(patches.reshape(per * cells, rays))
 
 
-def pack(tiles, slots, values_ref, row_ref, col_ref, out_ref):
+def pack(tiles, slots, values_ref, row_ref, col_ref, out_ref, send):
     per = row_ref.shape[1]
-    width = out_ref.shape[2]
+    parts, _, _, width = out_ref.shape
     row, col = row_ref[...], col_ref[...]
     shift = per.bit_length() - 1
     dest_row, dest_col = row >> shift, col >> shift
@@ -271,19 +296,24 @@
     choice = (
         lax.broadcasted_iota(jnp.int32, (tiles * slots, per), 0) == target_row
     ).astype(jnp.float32)
-    for c in range(4):
-        packed = jnp.dot(
-            choice,
-            values_ref[c],
-            precision=lax.Precision.HIGHEST,
-            preferred_element_type=jnp.float32,
-        )
-        out_ref[:, c * slots : (c + 1) * slots, :] = packed.reshape(tiles, slots, width)
     lane = lax.broadcasted_iota(jnp.int32, (per, width), 1)
     for tile in range(tiles):
         hit = (target_col == tile * slots + lane) & (lane < slots)
         mark = jnp.sum(jnp.where(hit, offset, 0.0), axis=0, keepdims=True) - 1.0
-        out_ref[tile, 4 * slots :, :] = jnp.broadcast_to(mark, (LABEL_ROWS, width))
+        for half in range(parts):
+            out_ref[half, tile, 4 * slots :, :] = jnp.broadcast_to(mark, (LABEL_ROWS, width))
+    for half in range(parts):
+        for c in range(4):
+            packed = jnp.dot(
+                choice,
+                values_ref[c, :, half * width : (half + 1) * width],
+                precision=lax.Precision.HIGHEST,
+                preferred_element_type=jnp.float32,
+            )
+            out_ref[half, :, c * slots : (c + 1) * slots, :] = packed.reshape(
+                tiles, slots, width
+            )
+        send(half)
 
 
 def place(slots, got_ref, out_ref):
@@ -307,27 +337,36 @@
         out_ref[:, c] = totals[c].reshape(quarters, share, width)
 
 
-def exchange(axis, count, source_ref, got_ref, send_sem, recv_sem):
-    me = lax.axis_index(axis)
-
-    def copy(piece, source, peer):
+class Exchange:
+    def __init__(self, axis, count, source_ref, got_ref, send_sem, recv_sem):
+        self.axis, self.me = axis, lax.axis_index(axis)
+        self.peers = [lax.rem(self.me + k, count) for k in range(1, count)]
+        self.refs = source_ref, got_ref, send_sem, recv_sem
+
+    def copy(self, half, piece, source, peer):
+        source_ref, got_ref, send_sem, recv_sem = self.refs
         return pltpu.make_async_remote_copy(
-            src_ref=source_ref.at[piece],
-            dst_ref=got_ref.at[source],
-            send_sem=send_sem.at[peer],
-            recv_sem=recv_sem.at[source],
-            device_id={axis: peer},
+            src_ref=source_ref.at[half, piece],
+            dst_ref=got_ref.at[half, source],
+            send_sem=send_sem.at[half, peer],
+            recv_sem=recv_sem.at[half, source],
+            device_id={self.axis: peer},
             device_id_type=MESH,
         )
 
-    peers = [lax.rem(me + k, count) for k in range(1, count)]
-    for peer in peers:
-        copy(peer, me, peer).start()
-    got_ref[me] = source_ref[me]
-    for peer in peers:
-        copy(me, peer, peer).wait_recv()
-    for peer in peers:
-        copy(peer, me, peer).wait_send()
+    def start(self, half):
+        source_ref, got_ref = self.refs[:2]
+        for peer in self.peers:
+            self.copy(half, peer, self.me, peer).start()
+        got_ref[half, self.me] = source_ref[half, self.me]
+
+    def arrive(self, half):
+        for peer in self.peers:
+            self.copy(half, self.me, peer, peer).wait_recv()
+
+    def drain(self, half):
+        for peer in self.peers:
+            self.copy(half, peer, self.me, peer).wait_send()
 
 
 def back_kernel(
@@ -340,18 +379,30 @@
         for k in range(1, count)
     ]
     greet(peers)
-    pack(tiles, slots, values_ref, row_ref, col_ref, packed)
-    exchange("tile", tiles, packed, got, tile_send, tile_recv)
-    place(slots, got, placed)
-    exchange("depth", quarters, placed, landed, depth_send, depth_recv)
-    out_ref[...] = landed[...]
+    over_tile = Exchange("tile", tiles, packed, got, tile_send, tile_recv)
+    over_depth = Exchange("depth", quarters, placed, landed, depth_send, depth_recv)
+    pack(tiles, slots, values_ref, row_ref, col_ref, packed, over_tile.start)
+    halves = range(packed.shape[0])
+    width = packed.shape[3]
+    for half in halves:
+        over_tile.arrive(half)
+        place(slots, got.at[half], placed.at[half])
+        over_depth.start(half)
+    for half in halves:
+        over_depth.arrive(half)
+        out_ref[:, :, :, half * width : (half + 1) * width] = landed[half]
+    for half in halves:
+        over_tile.drain(half)
+        over_depth.drain(half)
 
 
 def back(values, patch_slot, tiles, quarters, slots):
     _, per, width = values.shape
     dma = pltpu.SemaphoreType.DMA
     result = (quarters, 4, per // quarters, width)
-    block = (tiles, 4 * slots + LABEL_ROWS, width)
+    halves = width // LANES
+    piece = (halves, quarters, 4, per // quarters, LANES)
+    block = (halves, tiles, 4 * slots + LABEL_ROWS, LANES)
     return pl.pallas_call(
         functools.partial(back_kernel, tiles, quarters, slots),
         out_shape=jax.ShapeDtypeStruct(result, jnp.float32),
@@ -360,12 +411,12 @@
         scratch_shapes=[
             pltpu.VMEM(block, jnp.float32),
             pltpu.VMEM(block, jnp.float32),
-            pltpu.VMEM(result, jnp.float32),
-            pltpu.VMEM(result, jnp.float32),
-            dma((tiles,)),
-            dma((tiles,)),
-            dma((quarters,)),
-            dma((quarters,)),
+            pltpu.VMEM(piece, jnp.float32),
+            pltpu.VMEM(piece, jnp.float32),
+            dma((halves, tiles)),
+            dma((halves, tiles)),
+            dma((halves, quarters)),
+            dma((halves, quarters)),
         ],
         compiler_params=pltpu.CompilerParams(collective_id=1, has_side_effects=True),
         name="back",

time: 63.8 us -> 57.7 us (0.904)
  Pallas kernels: 60.3 us -> 54.2 us
    pallas_call x1, Pallas kernels: 27.8 us -> 21.1 us  [back(): pl.pallas_call(functools.partial(back_kernel, tiles, quarters, slots), ou...]
where the time goes in v2:
time: 57.7 us; the launch traced here: 57.6 us
  Pallas kernels  54.2 us (94%)
  local copies, waits for them, and re-layouts  3.36 us (6%)
    pallas_call x1, Pallas kernels, front(): pl.pallas_call(functools.partial(front_kernel, cells, quarters, 2.0 / (ce...  33.1 us
    pallas_call x1, Pallas kernels, back(): pl.pallas_call(functools.partial(back_kernel, tiles, quarters, slots), ou...  21.1 us
    reshape x2, local copies, waits for them, and re-layouts, local(): return final.transpose(2, 1, 0, 3).reshape(1, per // quarters, 4, rays)  2.01 us
    reshape x1, local copies, waits for them, and re-layouts, back(): patch_slot.reshape(per, 1)  1.36 us

profile of v2, /device:TPU:0, one launch (start us, length us, event | category | flops | bytes accessed | tf_op | source)
XLA Modules:
  0.0 57.6 jit_solution(11693037440221479044)
XLA Ops:
  0.0 1.4 %copy.4.col_ref = s32[64,1]{1,0:T(8,128)} copy(s32[64,1]{0,1:T(1,128)} %bitcast.6) | data formatting | bytes 512 | tf_op jit(solution)/shard_map/reshape | solution.py:423
  1.4 33.1 %front.1.values_ref = f32[4,64,256]{2,1,0:T(8,128)} custom-call(f32[1024,1024]{1,0:T(8,128)} %bitcast.4), custom_call_target="tpu_custom_call" | custom-call | tf_op jit(solution)/shard_map/front/pallas_call | solution.py:260
  34.5 21.1 %back.1 = f32[4,4,16,256]{3,2,1,0:T(8,128)} custom-call(f32[4,64,256]{2,1,0:T(8,128)} %front.1.values_ref, s32[1,64]{1,0:T(1,128)} %bitcast.7, s32[64,1]{1,0:T(8,128)} %copy.4.col_ref), custom_call_target="tpu_custom_call" | custom-call | tf_op jit(solution)/shard_map/back/pallas_call | solution.py:406
  55.6 1.1 %copy.7 = f32[16,4,4,256]{3,2,1,0:T(4,128)S(1)} copy(f32[16,4,4,256]{3,0,1,2:T(8,128)} %bitcast.5) | data formatting | bytes 524288 | tf_op jit(solution)/shard_map/reshape | solution.py:433
  56.7 0.9 %reshape.16 = f32[1,16,4,1024]{3,2,1,0:T(4,128)} reshape(f32[16,4,4,256]{3,2,1,0:T(4,128)S(1)} %copy.7) | data formatting | bytes 524288 | tf_op jit(solution)/shard_map/reshape | solution.py:433

commit v3 on v2

--- a/solution.py
+++ b/solution.py
@@ -125,10 +125,9 @@
     ones = functools.partial(jnp.ones, shape, jnp.float32)
     zeros = functools.partial(jnp.zeros, shape, jnp.float32)
 
-    @pl.loop(0, chunks)
-    def _(chunk):
-        quarter = chunk // halves
-        lanes = pl.ds(pl.multiple_of((chunk % halves) * LANES, LANES), LANES)
+    def interior(quarter, half):
+        chunk = quarter * halves + half
+        lanes = pl.ds(half * LANES, LANES)
 
         @pl.loop(0, per // rows)
         def _(step):
@@ -143,6 +142,13 @@
                 before, level, x = level, after, x_after
             for c in range(4):
                 part[quarter, c, patch_rows(step), lanes] = state[c].reshape(rows, LANES)
+
+    last = quarters - 1
+    near = (me < quarters // 2).astype(jnp.int32)
+    order = [k + near * (last - 2 * k) for k in range(quarters)]
+    for quarter in order[:last]:
+        for half in range(halves):
+            interior(quarter, half)
 
     @pl.when(me > 0)
     def _():
@@ -194,10 +200,10 @@
                 for c in range(4):
                     part[quarter, c, patch_rows(step), lanes] = total[c].reshape(rows, LANES)
 
-    last = quarters - 1
-    near = (me < quarters // 2).astype(jnp.int32)
-    for k in range(quarters):
-        quarter = k + near * (last - 2 * k)
+    for k, quarter in enumerate(order):
+        if k == last:
+            for half in range(halves):
+                interior(quarter, half)
         finish(quarter)
         if k < last:
             for side, end in enumerate((0, last)):
@@ -279,15 +285,18 @@
     )(patches.reshape(per * cells, rays))
 
 
-def pack(tiles, slots, values_ref, row_ref, col_ref, out_ref, send):
+def pack(tiles, slots, values_ref, row_ref, out_ref, send):
     per = row_ref.shape[1]
     parts, _, _, width = out_ref.shape
-    row, col = row_ref[...], col_ref[...]
+    row = row_ref[...]
+    down = lax.broadcasted_iota(jnp.int32, (per, per), 0)
+    across = lax.broadcasted_iota(jnp.int32, (per, per), 1)
+    col = jnp.sum(
+        jnp.where(down == across, row.astype(jnp.float32), 0.0), axis=1, keepdims=True
+    ).astype(jnp.int32)
     shift = per.bit_length() - 1
     dest_row, dest_col = row >> shift, col >> shift
     same = (dest_col == dest_row).astype(jnp.float32)
-    down = lax.broadcasted_iota(jnp.int32, (per, per), 0)
-    across = lax.broadcasted_iota(jnp.int32, (per, per), 1)
     rank_row = jnp.sum(jnp.where(down < across, same, 0.0), axis=0, keepdims=True)
     rank_col = jnp.sum(jnp.where(across < down, same, 0.0), axis=1, keepdims=True)
     target_row = dest_row * slots + rank_row.astype(jnp.int32)
@@ -370,7 +379,7 @@
 
 
 def back_kernel(
-    tiles, quarters, slots, values_ref, row_ref, col_ref, out_ref,
+    tiles, quarters, slots, values_ref, row_ref, out_ref,
     packed, got, placed, landed, tile_send, tile_recv, depth_send, depth_recv,
 ):
     peers = [
@@ -381,7 +390,7 @@
     greet(peers)
     over_tile = Exchange("tile", tiles, packed, got, tile_send, tile_recv)
     over_depth = Exchange("depth", quarters, placed, landed, depth_send, depth_recv)
-    pack(tiles, slots, values_ref, row_ref, col_ref, packed, over_tile.start)
+    pack(tiles, slots, values_ref, row_ref, packed, over_tile.start)
     halves = range(packed.shape[0])
     width = packed.shape[3]
     for half in halves:
@@ -390,7 +399,10 @@
         over_depth.start(half)
     for half in halves:
         over_depth.arrive(half)
-        out_ref[:, :, :, half * width : (half + 1) * width] = landed[half]
+        for quarter in range(quarters):
+            start = (quarter * len(halves) + half) * width
+            for c in range(4):
+                out_ref[:, c, start : start + width] = landed[half, quarter, c]
     for half in halves:
         over_tile.drain(half)
         over_depth.drain(half)
@@ -399,14 +411,14 @@
 def back(values, patch_slot, tiles, quarters, slots):
     _, per, width = values.shape
     dma = pltpu.SemaphoreType.DMA
-    result = (quarters, 4, per // quarters, width)
+    result = (per // quarters, 4, quarters * width)
     halves = width // LANES
     piece = (halves, quarters, 4, per // quarters, LANES)
     block = (halves, tiles, 4 * slots + LABEL_ROWS, LANES)
     return pl.pallas_call(
         functools.partial(back_kernel, tiles, quarters, slots),
         out_shape=jax.ShapeDtypeStruct(result, jnp.float32),
-        in_specs=[pl.BlockSpec(memory_space=pltpu.VMEM)] * 3,
+        in_specs=[pl.BlockSpec(memory_space=pltpu.VMEM)] * 2,
         out_specs=pl.BlockSpec(memory_space=pltpu.VMEM),
         scratch_shapes=[
             pltpu.VMEM(block, jnp.float32),
@@ -420,17 +432,17 @@
         ],
         compiler_params=pltpu.CompilerParams(collective_id=1, has_side_effects=True),
         name="back",
-    )(values, patch_slot.reshape(1, per), patch_slot.reshape(per, 1))
+    )(values, patch_slot.reshape(1, per))
 
 
 def local(patches, patch_slot):
-    per, _, rays = patches.shape
+    per = patches.shape[0]
     tiles = lax.axis_size("tile")
     quarters = lax.axis_size("depth")
     slots = -(-(3 * per // tiles) // 8) * 8
     values = front(patches, quarters)
     final = back(values, patch_slot, tiles, quarters, slots)
-    return final.transpose(2, 1, 0, 3).reshape(1, per // quarters, 4, rays)
+    return final.reshape((1,) + final.shape)
 
 
 def solution(mesh):

time: 57.7 us -> 56 us (0.971)
  local copies, waits for them, and re-layouts: 3.36 us -> 1.67 us
    reshape x3 -> x0, local copies, waits for them, and re-layouts: 3.36 us -> none  [the longest x2 2.01 us: local(): return final.transpose(2, 1, 0, 3).reshape(1, per // quarters, 4, rays)]
    unnamed x0 -> x1, local copies, waits for them, and re-layouts: none -> 1.67 us
where the time goes in v3:
time: 56 us; the launch traced here: 55.8 us
  Pallas kernels  54.1 us (97%)
  local copies, waits for them, and re-layouts  1.67 us (3%)
    pallas_call x1, Pallas kernels, front(): pl.pallas_call(functools.partial(front_kernel, cells, quarters, 2.0 / (ce...  33.1 us
    pallas_call x1, Pallas kernels, back(): pl.pallas_call(functools.partial(back_kernel, tiles, quarters, slots), ou...  21 us
    unnamed x1, local copies, waits for them, and re-layouts  1.67 us

profile of v3, /device:TPU:0, one launch (start us, length us, event | category | flops | bytes accessed | tf_op | source)
XLA Modules:
  0.0 55.8 jit_solution(13897787312562757658)
XLA Ops:
  0.0 33.1 %front.1.values_ref = f32[4,64,256]{2,1,0:T(8,128)} custom-call(f32[1024,1024]{1,0:T(8,128)} %bitcast.3), custom_call_target="tpu_custom_call" | custom-call | tf_op jit(solution)/shard_map/front/pallas_call | solution.py:266
  33.1 21.0 %back.1 = f32[16,4,1024]{2,1,0:T(4,128)} custom-call(f32[4,64,256]{2,1,0:T(8,128)} %front.1.values_ref, s32[1,64]{1,0:T(1,128)} %bitcast.5), custom_call_target="tpu_custom_call" | custom-call | tf_op jit(solution)/shard_map/back/pallas_call | solution.py:418
  54.2 1.7 %copy.4 = f32[1,16,4,1024]{3,2,1,0:T(4,128)} copy(f32[1,16,4,1024]{3,2,1,0:T(4,128)} %bitcast.4) | data formatting | bytes 524288
